TPU v7x, 256 devices: a whole 4x4x8 slice. The times are simulated.
256 devices in a mesh: row: 16 (over y, x), col: 16 (over z, core).
Axes of the slice: x: 4, y: 4, z: 8, core: 2. Of those that a mesh axis runs over, the one named last changes fastest.
Arguments:
- matrix: float32 [16384, 16384], P('row', 'col'), may hold values from 0 to 9.5, as said below
Outputs:
- factored: float32 [16384, 16384], P('row', 'col')
Inputs may be any that keep to these rules, and one draw needn't show every extreme that they name: `matrix`: symmetric positive definite once the block order is reverted.
All inputs are finite; a program needn't handle non-finite values.
Results may differ from a plain program's by a relative error of at most 0.0003.
Values sent between devices are 32-bit elements; how exact they have to be, the bound alone decides.
A program may use at most 128 MiB of HBM per device.

v0:
```python
import jax
import jax.numpy as jnp
from jax import lax
from jax.sharding import PartitionSpec as P

NB = 256
PANELS = 3


def from_root(shard, axis, root):
    mine = lax.axis_index(axis) == root
    return lax.psum(jnp.where(mine, shard, jnp.zeros_like(shard)), axis)


def solve_panel(factor, raw_rows):
    slots = raw_rows.shape[0]
    width = raw_rows.shape[1]
    flat = raw_rows.reshape(slots * width, width)
    solved = jax.scipy.linalg.solve_triangular(factor, flat.T, lower=True).T
    return solved.reshape(slots, width, width)


def subtract(part, panel_rows, column_rows):
    return part - jnp.einsum(
        "lan,mbn->lamb",
        panel_rows,
        column_rows,
        precision=lax.Precision.HIGHEST,
        preferred_element_type=jnp.float32,
    )


def body(matrix):
    grid_rows = lax.axis_size("row")
    grid_cols = lax.axis_size("col")
    row_slots = matrix.shape[0] // NB
    col_slots = matrix.shape[1] // NB
    stride = grid_cols // grid_rows
    my_row = lax.axis_index("row")
    my_col = lax.axis_index("col")
    blocks = matrix.reshape(row_slots, NB, col_slots, NB)
    row_ids = jnp.arange(row_slots, dtype=jnp.int32) * grid_rows + my_row
    col_ids = jnp.arange(col_slots, dtype=jnp.int32) * grid_cols + my_col
    carried = None
    for panel_at in range(PANELS):
        root_row = panel_at % grid_rows
        root_col = panel_at % grid_cols
        slot_row = panel_at // grid_rows
        slot_col = panel_at // grid_cols
        source = blocks[:, :, slot_col, :]
        below_mask = (row_ids > panel_at)[:, None, None]
        diag_block = from_root(source[slot_row], "row", root_row)
        factor = jnp.linalg.cholesky(diag_block)
        solved = jnp.where(below_mask, solve_panel(factor, source), 0.0)
        panel_rows = from_root(solved, "col", root_col)
        fetched = from_root(panel_rows, "row", my_col % grid_rows)
        column_rows = lax.dynamic_index_in_dim(
            fetched.reshape(col_slots, stride, NB, NB), my_col // grid_rows, 1, keepdims=False
        )
        owner_column = jnp.where((row_ids == panel_at)[:, None, None], factor[None], panel_rows)
        blocks = blocks.at[:, :, slot_col, :].set(
            jnp.where(my_col == root_col, owner_column, source)
        )
        blocks = subtract(blocks, panel_rows, column_rows)
        carried = None
    zero_mask = (row_ids[:, None] < col_ids[None, :]) & (row_ids[:, None] < PANELS)
    result = jnp.where(zero_mask[:, None, :, None], 0.0, blocks)
    return result.reshape(matrix.shape)


def solution(mesh):
    in_specs = (P("row", "col"),)
    out_specs = P("row", "col")
    return jax.shard_map(body, mesh=mesh, in_specs=in_specs, out_specs=out_specs, check_vma=False)
```

profile of v0, /device:TPU:32, one launch (start us, length us, event | category | flops | bytes accessed | tf_op | source)
XLA Modules:
  0.0 1180.5 jit_solution(10339150950592994072)
XLA Ops:
  6.5 5.6 reshape.239
  12.1 5.2 copy.29
  17.4 1.7 fusion.18
  19.1 2.9 slice.154
  22.2 94.0 %all-reduce.11.cloned.1.call-done = f32[256,256]{0,1:T(8,128)} async-done(((f32[256,256]{0,1:T(8,128)}), f32[256,256]{0,1:T(8,128)}) %all-reduce.11.cloned.1.call-update) | async-done | bytes 262160 | tf_op jit(solution)/shard_map/psum | solution.py:12
  118.2 11.7 cholesky.172
  130.0 9.8 custom-call.15
  140.3 11.7 cholesky.189
  154.1 4.2 while.9
  154.9 1.4 bitcast_dynamic-update-slice_fusion.7
  156.9 1.4 bitcast_dynamic-update-slice_fusion.7
  158.2 19.7 %custom-call.16 = f32[2,128,128]{1,2,0:T(8,128)S(1)} custom-call(f32[2,128,128]{2,1,0:T(8,128)S(1)} %get-tuple-element.63), custom_call_target="InvertDiagBlocksLowerTriangular" | custom-call | tf_op jit(solution)/shard_map/jit(_solve_triangular)/triangular_solve | solution.py:19
  182.3 108.2 %all-reduce.13.cloned.1.call-done = f32[4,256,256]{1,2,0:T(8,128)} async-done(((f32[4,256,256]{1,2,0:T(8,128)}), f32[4,256,256]{1,2,0:T(8,128)}) %all-reduce.13.cloned.1.call-update) | async-done | bytes 1048592 | tf_op jit(solution)/shard_map/psum | solution.py:12
  292.4 1.2 bitcast_dynamic-update-slice_fusion.3
  293.6 100.3 %all-reduce.15.cloned.1.call-done = f32[4,256,256]{1,2,0:T(8,128)} async-done(((f32[4,256,256]{1,2,0:T(8,128)}), f32[4,256,256]{1,2,0:T(8,128)}) %all-reduce.15.cloned.1.call-update) | async-done | bytes 1048592 | tf_op jit(solution)/shard_map/psum | solution.py:12
  393.9 5.8 convolution_subtract_fusion.1
  399.7 2.0 copy-done.1
  402.9 1.4 slice_bitcast_fusion.1
  404.7 91.4 %all-reduce.17.cloned.1.call-done = f32[256,256]{0,1:T(8,128)} async-done(((f32[256,256]{0,1:T(8,128)}), f32[256,256]{0,1:T(8,128)}) %all-reduce.17.cloned.1.call-update) | async-done | bytes 262160 | tf_op jit(solution)/shard_map/psum | solution.py:12
  498.2 11.7 cholesky.206
  510.0 9.8 custom-call.17
  520.3 11.7 cholesky.223
  534.7 4.2 while.10
  535.6 1.3 bitcast_dynamic-update-slice_fusion.8
  537.6 1.3 bitcast_dynamic-update-slice_fusion.8
  539.0 19.7 %custom-call.18 = f32[2,128,128]{1,2,0:T(8,128)S(1)} custom-call(f32[2,128,128]{2,1,0:T(8,128)S(1)} %get-tuple-element.64), custom_call_target="InvertDiagBlocksLowerTriangular" | custom-call | tf_op jit(solution)/shard_map/jit(_solve_triangular)/triangular_solve | solution.py:19
  561.7 1.2 select_select_fusion.1
  563.0 108.2 %all-reduce.19.cloned.1.call-done = f32[4,256,256]{1,2,0:T(8,128)} async-done(((f32[4,256,256]{1,2,0:T(8,128)}), f32[4,256,256]{1,2,0:T(8,128)}) %all-reduce.19.cloned.1.call-update) | async-done | bytes 1048592 | tf_op jit(solution)/shard_map/psum | solution.py:12
  672.8 1.2 fusion.3
  674.0 100.5 %all-reduce.21.cloned.1.call-done = f32[4,256,256]{1,2,0:T(8,128)} async-done(((f32[4,256,256]{1,2,0:T(8,128)}), f32[4,256,256]{1,2,0:T(8,128)}) %all-reduce.21.cloned.1.call-update) | async-done | bytes 1048592 | tf_op jit(solution)/shard_map/psum | solution.py:12
  774.5 5.8 convolution_subtract_fusion
  780.4 2.0 copy-done
  783.4 1.4 slice_bitcast_fusion
  785.1 91.7 %all-reduce.23.cloned.1.call-done = f32[256,256]{0,1:T(8,128)} async-done(((f32[256,256]{0,1:T(8,128)}), f32[256,256]{0,1:T(8,128)}) %all-reduce.23.cloned.1.call-update) | async-done | bytes 262160 | tf_op jit(solution)/shard_map/psum | solution.py:12
  878.9 11.7 cholesky.240
  890.7 9.8 custom-call.19
  901.0 11.7 cholesky.257
  915.4 4.3 while.11
  916.4 1.3 bitcast_dynamic-update-slice_fusion.9
  918.4 1.3 bitcast_dynamic-update-slice_fusion.9
  919.8 19.7 %custom-call.20 = f32[2,128,128]{1,2,0:T(8,128)S(1)} custom-call(f32[2,128,128]{2,1,0:T(8,128)S(1)} %get-tuple-element.65), custom_call_target="InvertDiagBlocksLowerTriangular" | custom-call | tf_op jit(solution)/shard_map/jit(_solve_triangular)/triangular_solve | solution.py:19
  942.5 1.2 select_select_fusion
  943.8 108.4 %all-reduce.25.cloned.1.call-done = f32[4,256,256]{1,2,0:T(8,128)} async-done(((f32[4,256,256]{1,2,0:T(8,128)}), f32[4,256,256]{1,2,0:T(8,128)}) %all-reduce.25.cloned.1.call-update) | async-done | bytes 1048592 | tf_op jit(solution)/shard_map/psum | solution.py:12
  1053.8 1.2 fusion.1
  1055.0 100.7 %all-reduce.27.cloned.1.call-done = f32[4,256,256]{1,2,0:T(8,128)} async-done(((f32[4,256,256]{1,2,0:T(8,128)}), f32[4,256,256]{1,2,0:T(8,128)}) %all-reduce.27.cloned.1.call-update) | async-done | bytes 1048592 | tf_op jit(solution)/shard_map/psum | solution.py:12
  1155.7 7.5 subtract_select_fusion
  1163.1 5.2 copy.53
  1168.4 5.2 copy.76
  (115 shorter events, 33.8 us)
Async XLA Ops:
  6.5 109.6 %all-reduce.11.cloned.1.call-start = ((), (), s32[]{:S(2)}) async-start(), calls=%async_computation | async-start | bytes 524288 | tf_op jit(solution)/shard_map/psum | solution.py:12
  19.1 271.4 %all-reduce.13.cloned.1.call-start = ((), (), s32[]{:S(2)}) async-start(), calls=%async_computation.1 | async-start | bytes 2097152 | tf_op jit(solution)/shard_map/psum | solution.py:12
  182.2 211.7 %all-reduce.15.cloned.1.call-start = ((), (), s32[]{:S(2)}) async-start(), calls=%async_computation.2 | async-start | bytes 2097152 | tf_op jit(solution)/shard_map/psum | solution.py:12
  290.4 2.0 copy-start.2
  291.5 204.6 %all-reduce.17.cloned.1.call-start = ((), (), s32[]{:S(2)}) async-start(), calls=%async_computation.3 | async-start | bytes 524288 | tf_op jit(solution)/shard_map/psum | solution.py:12
  399.7 2.0 copy-start.1
  402.5 268.7 %all-reduce.19.cloned.1.call-start = ((), (), s32[]{:S(2)}) async-start(), calls=%async_computation.4 | async-start | bytes 2097152 | tf_op jit(solution)/shard_map/psum | solution.py:12
  563.0 211.6 %all-reduce.21.cloned.1.call-start = ((), (), s32[]{:S(2)}) async-start(), calls=%async_computation.5 | async-start | bytes 2097152 | tf_op jit(solution)/shard_map/psum | solution.py:12
  671.2 1.6 copy-start.3
  672.3 204.5 %all-reduce.23.cloned.1.call-start = ((), (), s32[]{:S(2)}) async-start(), calls=%async_computation.6 | async-start | bytes 524288 | tf_op jit(solution)/shard_map/psum | solution.py:12
  780.3 2.0 copy-start
  783.1 269.1 %all-reduce.25.cloned.1.call-start = ((), (), s32[]{:S(2)}) async-start(), calls=%async_computation.7 | async-start | bytes 2097152 | tf_op jit(solution)/shard_map/psum | solution.py:12
  943.8 211.9 %all-reduce.27.cloned.1.call-start = ((), (), s32[]{:S(2)}) async-start(), calls=%async_computation.8 | async-start | bytes 2097152 | tf_op jit(solution)/shard_map/psum | solution.py:12
  1052.2 1.6 copy-start.4
Sparse Core Ops, SparseCore 0:
  19.2 96.8 all-reduce.10
  182.3 108.0 all-reduce.12
  293.7 100.1 all-reduce.14
  402.6 93.4 all-reduce.16
  563.1 108.0 all-reduce.18
  674.3 100.1 all-reduce.20
  783.2 93.5 all-reduce.22
  943.9 108.2 all-reduce.24
  1055.4 100.1 all-reduce.26
where the time goes:
time: 1190 us; the launch traced here: 1180 us
  waiting for transfers between devices  903 us (76%)
  other arithmetic  179 us (15%)
  local copies, waits for them, and re-layouts  50.7 us (4%)
  matrix products  27.3 us (2%)
  between operations  18 us (2%)
    psum x9, waiting for transfers between devices, from_root(): return lax.psum(jnp.where(mine, shard, jnp.zeros_like(shard)), axis)  903 us
    another operation x20, other arithmetic, body(): factor = jnp.linalg.cholesky(diag_block)  103 us
    another operation x7, other arithmetic, solve_panel(): solved = jax.scipy.linalg.solve_triangular(factor, flat.T, lower=True).T  59.1 us
  transfers between devices with their start and end apart: 9, of which 9 were waited for; matrix products, arithmetic and copies ran while one was open for 1% of the time, Pallas kernels for 0%

commit v1 on v0

--- a/solution.py
+++ b/solution.py
@@ -9,7 +9,8 @@
 
 def from_root(shard, axis, root):
     mine = lax.axis_index(axis) == root
-    return lax.psum(jnp.where(mine, shard, jnp.zeros_like(shard)), axis)
+    _turn_arrays = lambda s0, link_axis: lax.all_gather(s0, link_axis).sum(axis=0)
+    return _turn_arrays(jnp.where(mine, shard, jnp.zeros_like(shard)), axis)
 
 
 def solve_panel(factor, raw_rows):

time: 1190 us -> 1130 us (0.950)
  waiting for transfers between devices: 903 us -> 790 us
  other arithmetic: 179 us -> 227 us
    psum x9 -> x0, waiting for transfers between devices: 903 us -> none  [from_root(): return lax.psum(jnp.where(mine, shard, jnp.zeros_like(shard)), axis)]
    all_gather x0 -> x9, waiting for transfers between devices: none -> 790 us  [from_root(): lax.all_gather(s0, link_axis).sum(axis=0)]
    reduce_sum x0 -> x9, other arithmetic: none -> 49.4 us  [from_root(): lax.all_gather(s0, link_axis).sum(axis=0)]
where the time goes in v1:
time: 1130 us; the launch traced here: 1110 us
  waiting for transfers between devices  790 us (70%)
  other arithmetic  227 us (20%)
  local copies, waits for them, and re-layouts  44.1 us (4%)
  matrix products  33.7 us (3%)
  between operations  17.9 us (2%)
    all_gather x9, waiting for transfers between devices, from_root(): lax.all_gather(s0, link_axis).sum(axis=0)  790 us
    another operation x20, other arithmetic, body(): factor = jnp.linalg.cholesky(diag_block)  103 us
    another operation x7, other arithmetic, solve_panel(): solved = jax.scipy.linalg.solve_triangular(factor, flat.T, lower=True).T  59.1 us
    reduce_sum x9, other arithmetic, from_root(): lax.all_gather(s0, link_axis).sum(axis=0)  49.4 us
    dot_general x3, matrix products, subtract(): jnp.einsum('lan,mbn->lamb', panel_rows, column_rows, precision=lax.Precis...  26.7 us
  transfers between devices with their start and end apart: 9, of which 9 were waited for; matrix products, arithmetic and copies ran while one was open for 1% of the time, Pallas kernels for 0%

profile of v1, /device:TPU:32, one launch (start us, length us, event | category | flops | bytes accessed | tf_op | source)
XLA Modules:
  0.0 1114.5 jit_solution(9293597710394804832)
XLA Ops:
  6.5 5.6 reshape.347
  12.1 4.9 copy.27
  17.0 1.7 slice_select_fusion.2
  20.4 57.6 %all-gather.22.cloned.1.call-done = f32[16,256,1,256]{3,1,2,0:T(8,128)} async-done(((f32[1,256,1,256]{3,1,2,0:T(8,128)}), f32[16,256,1,256]{3,1,2,0:T(8,128)}) %all-gather.22.cloned.1.call-update) | async-done | bytes 4194320 | tf_op jit(solution)/shard_map/all_gather | solution.py:12
  78.0 2.5 reduce_sum.87
  80.7 11.7 %cholesky.172 = f32[128,128]{1,0:T(8,128)S(1)} custom-call(f32[128,128]{1,0:T(8,128)S(1)} %cholesky.270), custom_call_target="Cholesky" | custom-call | tf_op jit(solution)/shard_map/jit(cholesky)/cholesky | solution.py:54
  92.5 9.8 custom-call.15
  102.7 11.7 %cholesky.189 = f32[128,128]{1,0:T(8,128)S(1)} custom-call(f32[128,128]{1,0:T(8,128)S(1)} %convolution_subtract_fusion.7), custom_call_target="Cholesky" | custom-call | tf_op jit(solution)/shard_map/jit(cholesky)/cholesky | solution.py:54
  116.7 4.6 while.9
  117.8 1.4 bitcast_dynamic-update-slice_fusion.6
  119.8 1.4 bitcast_dynamic-update-slice_fusion.6
  121.3 19.7 %custom-call.16 = f32[2,128,128]{1,2,0:T(8,128)S(1)} custom-call(f32[2,128,128]{2,1,0:T(8,128)S(1)} %get-tuple-element.63), custom_call_target="InvertDiagBlocksLowerTriangular" | custom-call | tf_op jit(solution)/shard_map/jit(_solve_triangular)/triangular_solve | solution.py:20
  144.5 93.3 %all-gather.16.cloned.1.call-done = f32[16,4,256,256]{3,2,1,0:T(8,128)} async-done(((f32[1,4,256,256]{3,2,1,0:T(8,128)}), f32[16,4,256,256]{3,2,1,0:T(8,128)}) %all-gather.16.cloned.1.call-update) | async-done | bytes 16777232 | tf_op jit(solution)/shard_map/all_gather | solution.py:12
  237.8 7.0 reduce_sum.88
  246.9 2.4 fusion.11
  249.4 114.5 %all-gather.24.cloned.1.call-done = f32[64,256,256]{2,1,0:T(8,128)} async-done(((f32[4,256,256]{2,1,0:T(8,128)}), f32[64,256,256]{2,1,0:T(8,128)}) %all-gather.24.cloned.1.call-update) | async-done | bytes 16777232 | tf_op jit(solution)/shard_map/all_gather | solution.py:12
  363.8 7.0 reduce_sum.90
  370.8 8.7 convolution_subtract_fusion.1
  379.5 2.0 copy-done.1
  384.1 54.5 %all-gather.26.cloned.1.call-done = f32[16,256,1,256]{3,1,2,0:T(8,128)} async-done(((f32[1,256,1,256]{3,1,2,0:T(8,128)}), f32[16,256,1,256]{3,1,2,0:T(8,128)}) %all-gather.26.cloned.1.call-update) | async-done | bytes 4194320 | tf_op jit(solution)/shard_map/all_gather | solution.py:12
  438.7 2.5 reduce_sum.91
  441.4 11.7 %cholesky.206 = f32[128,128]{1,0:T(8,128)S(1)} custom-call(f32[128,128]{1,0:T(8,128)S(1)} %cholesky.273), custom_call_target="Cholesky" | custom-call | tf_op jit(solution)/shard_map/jit(cholesky)/cholesky | solution.py:54
  453.1 9.8 custom-call.17
  463.4 11.7 %cholesky.223 = f32[128,128]{1,0:T(8,128)S(1)} custom-call(f32[128,128]{1,0:T(8,128)S(1)} %convolution_subtract_fusion.6), custom_call_target="Cholesky" | custom-call | tf_op jit(solution)/shard_map/jit(cholesky)/cholesky | solution.py:54
  477.8 4.3 while.10
  482.1 19.7 %custom-call.18 = f32[2,128,128]{1,2,0:T(8,128)S(1)} custom-call(f32[2,128,128]{2,1,0:T(8,128)S(1)} %get-tuple-element.64), custom_call_target="InvertDiagBlocksLowerTriangular" | custom-call | tf_op jit(solution)/shard_map/jit(_solve_triangular)/triangular_solve | solution.py:20
  505.4 93.3 %all-gather.18.cloned.1.call-done = f32[16,4,256,256]{3,2,1,0:T(8,128)} async-done(((f32[1,4,256,256]{3,2,1,0:T(8,128)}), f32[16,4,256,256]{3,2,1,0:T(8,128)}) %all-gather.18.cloned.1.call-update) | async-done | bytes 16777232 | tf_op jit(solution)/shard_map/all_gather | solution.py:12
  598.7 7.0 reduce_sum.92
  607.8 2.4 fusion.7
  610.3 114.5 %all-gather.28.cloned.1.call-done = f32[64,256,256]{2,1,0:T(8,128)} async-done(((f32[4,256,256]{2,1,0:T(8,128)}), f32[64,256,256]{2,1,0:T(8,128)}) %all-gather.28.cloned.1.call-update) | async-done | bytes 16777232 | tf_op jit(solution)/shard_map/all_gather | solution.py:12
  724.7 7.0 reduce_sum.94
  731.7 8.7 convolution_subtract_fusion
  740.4 2.0 copy-done
  745.3 54.3 %all-gather.30.cloned.1.call-done = f32[16,256,1,256]{3,1,2,0:T(8,128)} async-done(((f32[1,256,1,256]{3,1,2,0:T(8,128)}), f32[16,256,1,256]{3,1,2,0:T(8,128)}) %all-gather.30.cloned.1.call-update) | async-done | bytes 4194320 | tf_op jit(solution)/shard_map/all_gather | solution.py:12
  799.6 2.5 reduce_sum.95
  802.3 11.7 %cholesky.240 = f32[128,128]{1,0:T(8,128)S(1)} custom-call(f32[128,128]{1,0:T(8,128)S(1)} %cholesky.276), custom_call_target="Cholesky" | custom-call | tf_op jit(solution)/shard_map/jit(cholesky)/cholesky | solution.py:54
  814.0 9.8 custom-call.19
  824.3 11.7 %cholesky.257 = f32[128,128]{1,0:T(8,128)S(1)} custom-call(f32[128,128]{1,0:T(8,128)S(1)} %convolution_subtract_fusion.5), custom_call_target="Cholesky" | custom-call | tf_op jit(solution)/shard_map/jit(cholesky)/cholesky | solution.py:54
  838.8 4.2 while.11
  843.0 19.7 %custom-call.20 = f32[2,128,128]{1,2,0:T(8,128)S(1)} custom-call(f32[2,128,128]{2,1,0:T(8,128)S(1)} %get-tuple-element.65), custom_call_target="InvertDiagBlocksLowerTriangular" | custom-call | tf_op jit(solution)/shard_map/jit(_solve_triangular)/triangular_solve | solution.py:20
  866.3 93.3 %all-gather.20.cloned.1.call-done = f32[16,4,256,256]{3,2,1,0:T(8,128)} async-done(((f32[1,4,256,256]{3,2,1,0:T(8,128)}), f32[16,4,256,256]{3,2,1,0:T(8,128)}) %all-gather.20.cloned.1.call-update) | async-done | bytes 16777232 | tf_op jit(solution)/shard_map/all_gather | solution.py:12
  959.6 7.0 reduce_sum.96
  968.8 2.4 fusion.3
  971.2 114.4 %all-gather.32.cloned.1.call-done = f32[64,256,256]{2,1,0:T(8,128)} async-done(((f32[4,256,256]{2,1,0:T(8,128)}), f32[64,256,256]{2,1,0:T(8,128)}) %all-gather.32.cloned.1.call-update) | async-done | bytes 16777232 | tf_op jit(solution)/shard_map/all_gather | solution.py:12
  1085.6 7.0 reduce_sum.98
  1092.6 9.4 subtract_select_fusion
  1102.0 2.7 copy.44
  1104.7 3.0 copy.61
  (117 shorter events, 39.0 us)
Async XLA Ops:
  6.5 71.5 %all-gather.22.cloned.1.call-start = ((), (), s32[]{:S(2)}) async-start(), calls=%async_computation.3 | async-start | bytes 4456448 | tf_op jit(solution)/shard_map/all_gather | solution.py:12
  18.7 219.1 %all-gather.16.cloned.1.call-start = ((), (), s32[]{:S(2)}) async-start(), calls=%async_computation | async-start | bytes 17825792 | tf_op jit(solution)/shard_map/all_gather | solution.py:12
  144.5 219.4 %all-gather.24.cloned.1.call-start = ((), (), s32[]{:S(2)}) async-start(), calls=%async_computation.4 | async-start | bytes 17825792 | tf_op jit(solution)/shard_map/all_gather | solution.py:12
  246.9 191.8 %all-gather.26.cloned.1.call-start = ((), (), s32[]{:S(2)}) async-start(), calls=%async_computation.5 | async-start | bytes 4456448 | tf_op jit(solution)/shard_map/all_gather | solution.py:12
  379.5 2.0 copy-start.1
  382.3 216.5 %all-gather.18.cloned.1.call-start = ((), (), s32[]{:S(2)}) async-start(), calls=%async_computation.1 | async-start | bytes 17825792 | tf_op jit(solution)/shard_map/all_gather | solution.py:12
  505.3 219.4 %all-gather.28.cloned.1.call-start = ((), (), s32[]{:S(2)}) async-start(), calls=%async_computation.6 | async-start | bytes 17825792 | tf_op jit(solution)/shard_map/all_gather | solution.py:12
  607.8 191.8 %all-gather.30.cloned.1.call-start = ((), (), s32[]{:S(2)}) async-start(), calls=%async_computation.7 | async-start | bytes 4456448 | tf_op jit(solution)/shard_map/all_gather | solution.py:12
  740.4 2.0 copy-start
  743.2 216.4 %all-gather.20.cloned.1.call-start = ((), (), s32[]{:S(2)}) async-start(), calls=%async_computation.2 | async-start | bytes 17825792 | tf_op jit(solution)/shard_map/all_gather | solution.py:12
  866.2 219.4 %all-gather.32.cloned.1.call-start = ((), (), s32[]{:S(2)}) async-start(), calls=%async_computation.8 | async-start | bytes 17825792 | tf_op jit(solution)/shard_map/all_gather | solution.py:12
Sparse Core Ops, SparseCore 0:
  18.8 59.1 all-gather.21
  144.6 93.2 all-gather.15
  247.0 116.7 all-gather.23
  382.4 56.2 all-gather.25
  505.5 93.2 all-gather.17
  607.9 116.7 all-gather.27
  743.3 56.2 all-gather.29
  866.3 93.2 all-gather.19
  968.8 116.7 all-gather.31
